TPU v7x, 32 devices: a whole 2x2x4 slice. The times are simulated.
32 devices in a mesh: grp: 1, row: 32 (over z, y, x, core).
Axes of the slice: x: 2, y: 2, z: 4, core: 2. Of those that a mesh axis runs over, the one named last changes fastest.
Arguments:
- homolog_matrix: bfloat16 [64, 128, 256], P(('grp', 'row')), may hold values from -6 to 6
- alignment_mask: int32 [64, 128], P(('grp', 'row')), may hold values from 0 to 1, as said below
- pair_state_input: bfloat16 [128, 128, 128], P(('grp', 'row')), may hold values from -3 to 3
- chain_label: int32 [128], P('grp'), may hold values from 0 to 3, never falling along the last dimension, each value on 1 to 64 neighbouring positions
- residue_number_index: int32 [128], P('grp'), may hold values from 1 to 382, as said below
- relative_position_table: float32 [66, 128], replicated, may hold values from -3 to 3
- tensor_factor_coefficients: bfloat16 [256, 64], replicated, may hold values from -0.375 to 0.375
- outer_output_weight: bfloat16 [1024, 128], replicated, may hold values from -3 to 3
- scorer_entry_coefficients: bfloat16 [256, 1024], replicated, may hold values from -0.375 to 0.375
- scorer_final_coefficients: bfloat16 [256, 256], replicated, may hold values from -0.375 to 0.375
- pair_bias_weight: bfloat16 [128, 8], replicated
- triangle_input_weight: bfloat16 [128, 512], replicated, may hold values from -0.5 to 0.5
- triangle_output_gate: bfloat16 [128, 128], replicated, may hold values from -1.5 to 1.5
- triangle_output_weight: bfloat16 [128, 128], replicated, may hold values from -1.796875 to 1.796875
Outputs:
- homolog_revised: bfloat16 [64, 128, 256], P(('grp', 'row'))
- pair_state_output: bfloat16 [128, 128, 128], P(('grp', 'row'))
Inputs may be any that keep to these rules, and one draw needn't show every extreme that they name: `alignment_mask`: 1 marks a live entry of an MSA row. `chain_label`: chain ids never fall along the residues; a chain holds at most 64 residues. `residue_number_index`: residue numbers strictly increase along the residues.
All inputs are finite; a program needn't handle non-finite values.
Results may differ from a plain program's by a relative error of at most 0.03.
Values may be sent and summed in bfloat16 or wider, within the bound.
A program may use at most 128 MiB of HBM per device.

v0:
```python
import jax
import jax.numpy as jnp
from jax import lax
from jax.sharding import PartitionSpec as P

REL_MAX = 32


def layer_normalize(values):
    centre = jnp.mean(values, axis=-1, keepdims=True)
    shifted = values - centre
    spread = jnp.mean(shifted * shifted, axis=-1, keepdims=True)
    return shifted * lax.rsqrt(spread + 1e-05)


def on_device(
    homolog_matrix,
    alignment_mask,
    pair_state_input,
    chain_label,
    residue_number_index,
    relative_position_table,
    tensor_factor_coefficients,
    outer_output_weight,
    scorer_entry_coefficients,
    scorer_final_coefficients,
    pair_bias_weight,
    triangle_input_weight,
    triangle_output_gate,
    triangle_output_weight,
):
    sequence_local_rows = homolog_matrix.shape[0]
    residue_total = homolog_matrix.shape[1]
    alignment_width = homolog_matrix.shape[2]
    res_local = pair_state_input.shape[0]
    pair_width = pair_state_input.shape[2]
    opm_width = tensor_factor_coefficients.shape[1] // 2
    head_total = pair_bias_weight.shape[1]
    head_channel_width = alignment_width // head_total
    tri_width = triangle_input_weight.shape[1] // 4
    table_rows = relative_position_table.shape[0]
    row_start = lax.axis_index("row") * res_local
    contract = (((0,), (0,)), ((), ()))
    active_entry_mask = alignment_mask.astype(jnp.float32)
    homolog_rescaled = layer_normalize(homolog_matrix.astype(jnp.float32)).astype(jnp.bfloat16)
    homolog_lines_merged = homolog_rescaled.reshape(
        sequence_local_rows * residue_total, alignment_width
    )
    projected_rows = jnp.dot(
        homolog_lines_merged, tensor_factor_coefficients, preferred_element_type=jnp.float32
    ).reshape(sequence_local_rows, residue_total, 2 * opm_width)
    left_factor = (
        (projected_rows[..., :opm_width] * active_entry_mask[..., None])
        .astype(jnp.bfloat16)
        .reshape(sequence_local_rows, residue_total * opm_width)
    )
    right_factor = (
        (projected_rows[..., opm_width:] * active_entry_mask[..., None])
        .astype(jnp.bfloat16)
        .reshape(sequence_local_rows, residue_total * opm_width)
    )
    live_weights = active_entry_mask.astype(jnp.bfloat16)
    left_all, right_all, live_all = (
        lax.all_gather(left_factor, "row", axis=0, tiled=True),
        lax.all_gather(right_factor, "row", axis=0, tiled=True),
        lax.all_gather(live_weights, "row", axis=0, tiled=True),
    )
    left_cols = lax.dynamic_slice_in_dim(left_all, row_start * opm_width, res_local * opm_width, 1)
    live_cols = lax.dynamic_slice_in_dim(live_all, row_start, res_local, 1)
    outer_sum = lax.dot_general(left_cols, right_all, contract, preferred_element_type=jnp.float32)
    pair_count = lax.dot_general(live_cols, live_all, contract, preferred_element_type=jnp.float32)
    outer_flat = outer_sum.reshape(res_local, opm_width, residue_total, opm_width).transpose(
        0, 2, 1, 3
    )
    outer_flat = outer_flat.reshape(res_local * residue_total, opm_width * opm_width).astype(
        jnp.bfloat16
    )
    opm_update = jnp.dot(
        outer_flat, outer_output_weight, preferred_element_type=jnp.float32
    ).reshape(res_local, residue_total, pair_width)
    opm_update = opm_update / (0.001 + pair_count[..., None])
    chain_rows = lax.dynamic_slice_in_dim(chain_label, row_start, res_local, 0)
    index_rows = lax.dynamic_slice_in_dim(residue_number_index, row_start, res_local, 0)
    same_chain = chain_rows[:, None] == chain_label[None, :]
    offsets = (
        jnp.clip(index_rows[:, None] - residue_number_index[None, :], -REL_MAX, REL_MAX) + REL_MAX
    )
    bin_index = jnp.where(same_chain, offsets, 2 * REL_MAX + 1)
    one_hot = (
        (bin_index[..., None] == jnp.arange(table_rows, dtype=jnp.int32))
        .astype(jnp.float32)
        .reshape(-1, table_rows)
    )
    position_term = jnp.dot(
        one_hot, relative_position_table, precision=lax.Precision.HIGHEST
    ).reshape(res_local, residue_total, pair_width)
    updated = (pair_state_input.astype(jnp.float32) + position_term + opm_update).astype(
        jnp.bfloat16
    )
    pair_norm = layer_normalize(updated.astype(jnp.float32)).astype(jnp.bfloat16)
    pair_flat = pair_norm.reshape(res_local * residue_total, pair_width)
    head_bias = jnp.dot(pair_flat, pair_bias_weight, preferred_element_type=jnp.float32).astype(
        jnp.bfloat16
    )
    head_bias = head_bias.reshape(res_local, residue_total, head_total).transpose(2, 0, 1)
    full_bias = lax.all_gather(head_bias, "row", axis=1, tiled=True)
    tri_projected = jnp.dot(pair_flat, triangle_input_weight, preferred_element_type=jnp.float32)
    tri_left = (
        jax.nn.sigmoid(tri_projected[:, :tri_width]) * tri_projected[:, tri_width : 2 * tri_width]
    ).astype(jnp.bfloat16)
    tri_right = (
        jax.nn.sigmoid(tri_projected[:, 2 * tri_width : 3 * tri_width])
        * tri_projected[:, 3 * tri_width :]
    ).astype(jnp.bfloat16)
    tri_left = tri_left.reshape(res_local, residue_total, tri_width).transpose(2, 0, 1)
    tri_right = tri_right.reshape(res_local, residue_total, tri_width).transpose(2, 0, 1)
    left_channels, right_channels = (
        lax.all_to_all(tri_left, "row", split_axis=0, concat_axis=1, tiled=True),
        lax.all_to_all(tri_right, "row", split_axis=0, concat_axis=1, tiled=True),
    )
    channel_sum = jnp.einsum(
        "cki,ckj->cij", left_channels, right_channels, preferred_element_type=jnp.float32
    ).astype(jnp.bfloat16)
    row_sum = lax.all_to_all(channel_sum, "row", split_axis=1, concat_axis=0, tiled=True)
    tri_sum = row_sum.transpose(1, 2, 0)
    tri_normed = (
        layer_normalize(tri_sum.astype(jnp.float32))
        .astype(jnp.bfloat16)
        .reshape(res_local * residue_total, tri_width)
    )
    tri_gating = jax.nn.sigmoid(
        jnp.dot(pair_flat, triangle_output_gate, preferred_element_type=jnp.float32)
    )
    pair_state_output = updated.astype(jnp.float32).reshape(
        res_local * residue_total, pair_width
    ) + tri_gating * jnp.dot(tri_normed, triangle_output_weight, preferred_element_type=jnp.float32)
    pair_state_output = pair_state_output.astype(jnp.bfloat16).reshape(
        res_local, residue_total, pair_width
    )
    scorer_mapped_lines = jnp.dot(
        homolog_lines_merged, scorer_entry_coefficients, preferred_element_type=jnp.float32
    )
    asking_vectors = (
        scorer_mapped_lines[:, :alignment_width]
        .astype(jnp.bfloat16)
        .reshape(sequence_local_rows, residue_total, head_total, head_channel_width)
    )
    lookup_lines = (
        scorer_mapped_lines[:, alignment_width : 2 * alignment_width]
        .astype(jnp.bfloat16)
        .reshape(sequence_local_rows, residue_total, head_total, head_channel_width)
    )
    content_lines = (
        scorer_mapped_lines[:, 2 * alignment_width : 3 * alignment_width]
        .astype(jnp.bfloat16)
        .reshape(sequence_local_rows, residue_total, head_total, head_channel_width)
    )
    sigmoid_factor = (
        scorer_mapped_lines[:, 3 * alignment_width :]
        .astype(jnp.bfloat16)
        .reshape(sequence_local_rows, residue_total, head_total, head_channel_width)
    )
    mask_term = 1000000000.0 * (active_entry_mask - 1.0)
    score_scale = head_channel_width ** (-0.5)

    def attend(row_inputs):
        query_row, key_row, value_row, gate_row, mask_row = row_inputs
        scores = (
            jnp.einsum("ihd,jhd->hij", query_row, key_row, preferred_element_type=jnp.float32)
            * score_scale
        )
        scores = scores + full_bias.astype(jnp.float32) + mask_row[None, None, :]
        weights = jax.nn.softmax(scores, axis=-1).astype(jnp.bfloat16)
        attended = jnp.einsum(
            "hij,jhd->ihd", weights, value_row, preferred_element_type=jnp.float32
        )
        return (jax.nn.sigmoid(gate_row.astype(jnp.float32)) * attended).astype(jnp.bfloat16)

    sigmoid_scaled_lines = lax.map(
        attend, (asking_vectors, lookup_lines, content_lines, sigmoid_factor, mask_term)
    )
    homolog_revised = homolog_matrix.astype(jnp.float32).reshape(
        sequence_local_rows * residue_total, alignment_width
    ) + jnp.dot(
        sigmoid_scaled_lines.reshape(sequence_local_rows * residue_total, alignment_width),
        scorer_final_coefficients,
        preferred_element_type=jnp.float32,
    )
    homolog_revised = homolog_revised.astype(jnp.bfloat16).reshape(
        sequence_local_rows, residue_total, alignment_width
    )
    return (homolog_revised, pair_state_output)


def solution(mesh):
    return jax.shard_map(
        on_device,
        mesh=mesh,
        in_specs=(
            P(("grp", "row"), None, None),
            P(("grp", "row"), None),
            P(("grp", "row"), None, None),
            P("grp"),
            P("grp"),
            P(),
            P(),
            P(),
            P(),
            P(),
            P(),
            P(),
            P(),
            P(),
        ),
        out_specs=(P(("grp", "row"), None, None), P(("grp", "row"), None, None)),
        check_vma=False,
    )
```

profile of v0, /device:TPU:0, one launch (start us, length us, event | category | flops | bytes accessed | tf_op | source)
XLA Modules:
  0.0 210.1 jit_solution(4078920670390650498)
XLA Ops:
  0.6 1.1 convert_reduce_fusion
  1.7 1.1 multiply_reduce_fusion.2
  2.8 1.0 multiply_convert_fusion.2
  3.9 0.7 convert_bitcast_fusion
  4.6 0.9 fusion.51
  5.8 44.6 %all-gather = bf16[32,2,4096]{2,1,0:T(2,128)(2,1)S(1)} all-gather(bf16[1,2,4096]{2,1,0:T(2,128)(2,1)S(1)} %reshape.208), channel_id=1, replica_groups=mesh['grp'=1,'row'=32] {'row'}, dimensions={0}, use_global_device_ids=true | all-gather | bytes 540672 | tf_op jit(solution)/shard_map/all_gather | solution.py:64
  50.9 38.1 %all-gather.1 = bf16[32,2,4096]{2,1,0:T(2,128)(2,1)S(1)} all-gather(bf16[1,2,4096]{2,1,0:T(2,128)(2,1)S(1)} %reshape.210), channel_id=1, replica_groups=mesh['grp'=1,'row'=32] {'row'}, dimensions={0}, use_global_device_ids=true | all-gather | bytes 540672 | tf_op jit(solution)/shard_map/all_gather | solution.py:65
  89.2 0.5 convolution_convert_fusion
  89.7 4.5 %convert_element_type.106 = bf16[4,32,128,32]{3,2,1,0:T(8,128)(2,1)} reshape(bf16[128,4096]{1,0:T(8,128)(2,1)S(1)} %convolution_convert_fusion) | data formatting | bytes 2097152 | tf_op jit(solution)/shard_map/convert_element_type | solution.py:75
  94.1 3.6 %copy.75 = bf16[4,128,32,32]{1,3,2,0:T(8,128)(2,1)S(1)} copy(bf16[4,128,32,32]{3,1,2,0:T(8,128)(2,1)} %bitcast.135) | data formatting | bytes 2097152 | tf_op jit(solution)/shard_map/convert_element_type | solution.py:75
  97.7 37.9 %all-gather.2 = bf16[32,2,128]{2,1,0:T(2,128)(2,1)S(1)} all-gather(bf16[1,2,128]{2,1,0:T(2,128)(2,1)S(1)} %get-tuple-element.101), channel_id=1, replica_groups=mesh['grp'=1,'row'=32] {'row'}, dimensions={0}, use_global_device_ids=true | all-gather | bytes 16896 | tf_op jit(solution)/shard_map/all_gather | solution.py:66
  136.1 0.5 convolution_divide_fusion
  136.6 0.5 fusion.63
  137.6 0.3 fusion.64
  138.0 0.8 copy.83
  138.8 2.6 %all-to-all-start = ((bf16[128,4,128]{2,1,0:T(4,128)(2,1)}), bf16[128,4,128]{2,1,0:T(4,128)(2,1)S(1)}, u32[]{:S(2)}, u32[]{:S(2)}) async-start(bf16[128,4,128]{2,1,0:T(4,128)(2,1)} %bitcast.22), calls=%async_computation | async-start | bytes 262144 | tf_op jit(solution)/shard_map/all_to_all | solution.py:118
  141.5 0.3 convolution_convert_fusion.1
  141.9 42.5 %all_gather.15 = bf16[8,128,128]{2,0,1:T(8,128)(2,1)S(1)} all-gather(bf16[8,4,128]{2,0,1:T(8,128)(2,1)S(1)} %fusion.35), channel_id=1, replica_groups=mesh['grp'=1,'row'=32] {'row'}, dimensions={1}, use_global_device_ids=true | all-gather | bytes 270336 | tf_op jit(solution)/shard_map/all_gather | solution.py:106
  184.4 0.8 copy.86
  186.1 2.6 %all-to-all-start.1 = ((bf16[128,4,128]{2,1,0:T(4,128)(2,1)}), bf16[128,4,128]{2,1,0:T(4,128)(2,1)S(1)}, u32[]{:S(2)}, u32[]{:S(2)}) async-start(bf16[128,4,128]{2,1,0:T(4,128)(2,1)} %bitcast.27), calls=%async_computation.1 | async-start | bytes 262144 | tf_op jit(solution)/shard_map/all_to_all | solution.py:119
  188.8 2.0 while.10
  188.8 0.3 fusion.101
  189.1 0.4 fusion.100
  189.5 0.3 fusion.102
  189.8 0.3 fusion.101
  190.1 0.4 fusion.100
  190.9 6.1 %all-to-all-done.1 = bf16[128,4,128]{2,1,0:T(4,128)(2,1)S(1)} async-done(((bf16[128,4,128]{2,1,0:T(4,128)(2,1)}), bf16[128,4,128]{2,1,0:T(4,128)(2,1)S(1)}, u32[]{:S(2)}, u32[]{:S(2)}) %all-to-all-start.1) | async-done | bytes 131104 | tf_op jit(solution)/shard_map/all_to_all | solution.py:119
  197.3 0.8 copy.90
  198.1 2.6 %all-to-all-start.2 = ((bf16[4,128,128]{2,0,1:T(4,128)(2,1)}), bf16[4,128,128]{2,0,1:T(4,128)(2,1)S(1)}, u32[]{:S(2)}, u32[]{:S(2)}) async-start(bf16[4,128,128]{2,0,1:T(4,128)(2,1)} %copy.90), calls=%async_computation.2 | async-start | bytes 262144 | tf_op jit(solution)/shard_map/all_to_all | solution.py:124
  201.1 0.9 fusion.33
  202.0 6.9 %all-to-all-done.2 = bf16[4,128,128]{2,0,1:T(4,128)(2,1)S(1)} async-done(((bf16[4,128,128]{2,0,1:T(4,128)(2,1)}), bf16[4,128,128]{2,0,1:T(4,128)(2,1)S(1)}, u32[]{:S(2)}, u32[]{:S(2)}) %all-to-all-start.2) | async-done | bytes 131104 | tf_op jit(solution)/shard_map/all_to_all | solution.py:124
  209.2 0.8 fusion.34
  (79 shorter events, 4.5 us)
Async XLA Ops:
  0.6 140.9 %copy-start = (bf16[256,1024]{1,0:T(8,128)(2,1)S(1)}, bf16[256,1024]{1,0:T(8,128)(2,1)}, u32[]{:S(2)}) copy-start(bf16[256,1024]{1,0:T(8,128)(2,1)} %param.24) | copy-start | bytes 1572868
  89.6 46.2 %copy-start.10 = (s32[128]{0:T(128)S(1)}, s32[128]{0:T(128)}, u32[]{:S(2)}) copy-start(s32[128]{0:T(128)} %param.19) | copy-start | bytes 1540
  89.6 46.3 %copy-start.9 = (s32[128]{0:T(128)S(1)}, s32[128]{0:T(128)}, u32[]{:S(2)}) copy-start(s32[128]{0:T(128)} %param.20) | copy-start | bytes 1540
  89.6 46.4 %copy-start.11 = (bf16[1024,128]{1,0:T(8,128)(2,1)S(1)}, bf16[1024,128]{1,0:T(8,128)(2,1)}, u32[]{:S(2)}) copy-start(bf16[1024,128]{1,0:T(8,128)(2,1)} %param.23) | copy-start | bytes 786436
  94.1 42.5 %copy-start.3 = (bf16[4,128,128]{2,1,0:T(8,128)(2,1)S(1)}, bf16[4,128,128]{2,1,0:T(8,128)(2,1)}, u32[]{:S(2)}) copy-start(bf16[4,128,128]{2,1,0:T(8,128)(2,1)} %param.18) | copy-start | bytes 393220
  94.1 42.5 %copy-start.5 = (f32[66,128]{1,0:T(8,128)S(1)}, f32[66,128]{1,0:T(8,128)}, u32[]{:S(2)}) copy-start(f32[66,128]{1,0:T(8,128)} %param.21) | copy-start | bytes 101380
  94.1 43.4 %copy-start.2 = (bf16[128,512]{1,0:T(8,128)(2,1)S(1)}, bf16[128,512]{1,0:T(8,128)(2,1)}, u32[]{:S(2)}) copy-start(bf16[128,512]{1,0:T(8,128)(2,1)} %param.27) | copy-start | bytes 393220
  97.7 43.7 %copy-start.8 = (bf16[128,8]{0,1:T(8,128)(2,1)S(1)}, bf16[128,8]{0,1:T(8,128)(2,1)}, u32[]{:S(2)}) copy-start(bf16[128,8]{0,1:T(8,128)(2,1)} %param.26) | copy-start | bytes 6148
  137.8 48.3 %copy-start.7 = (s32[2,128]{1,0:T(2,128)S(1)}, s32[2,128]{1,0:T(2,128)}, u32[]{:S(2)}) copy-start(s32[2,128]{1,0:T(2,128)} %param.17) | copy-start | bytes 3076
  138.8 47.3 %all-to-all-start = ((bf16[128,4,128]{2,1,0:T(4,128)(2,1)}), bf16[128,4,128]{2,1,0:T(4,128)(2,1)S(1)}, u32[]{:S(2)}, u32[]{:S(2)}) async-start(bf16[128,4,128]{2,1,0:T(4,128)(2,1)} %bitcast.22), calls=%async_computation | async-start | bytes 262144 | tf_op jit(solution)/shard_map/all_to_all | solution.py:118
  186.1 10.8 %all-to-all-start.1 = ((bf16[128,4,128]{2,1,0:T(4,128)(2,1)}), bf16[128,4,128]{2,1,0:T(4,128)(2,1)S(1)}, u32[]{:S(2)}, u32[]{:S(2)}) async-start(bf16[128,4,128]{2,1,0:T(4,128)(2,1)} %bitcast.27), calls=%async_computation.1 | async-start | bytes 262144 | tf_op jit(solution)/shard_map/all_to_all | solution.py:119
  188.7 11.9 %copy-start.12 = (bf16[128,128]{1,0:T(8,128)(2,1)S(1)}, bf16[128,128]{1,0:T(8,128)(2,1)}, u32[]{:S(2)}) copy-start(bf16[128,128]{1,0:T(8,128)(2,1)} %param.28) | copy-start | bytes 98308
  188.8 12.3 %copy-start.1 = (bf16[2,128,256]{2,1,0:T(8,128)(2,1)S(1)}, bf16[2,128,256]{2,1,0:T(8,128)(2,1)}, u32[]{:S(2)}) copy-start(bf16[2,128,256]{2,1,0:T(8,128)(2,1)} %param.16) | copy-start | bytes 393220
  188.8 12.3 %copy-start.4 = (bf16[256,256]{1,0:T(8,128)(2,1)S(1)}, bf16[256,256]{1,0:T(8,128)(2,1)}, u32[]{:S(2)}) copy-start(bf16[256,256]{1,0:T(8,128)(2,1)} %param.25) | copy-start | bytes 393220
  190.8 18.5 %copy-start.6 = (bf16[128,128]{1,0:T(8,128)(2,1)S(1)}, bf16[128,128]{1,0:T(8,128)(2,1)}, u32[]{:S(2)}) copy-start(bf16[128,128]{1,0:T(8,128)(2,1)} %param.29) | copy-start | bytes 98308
  198.1 10.8 %all-to-all-start.2 = ((bf16[4,128,128]{2,0,1:T(4,128)(2,1)}), bf16[4,128,128]{2,0,1:T(4,128)(2,1)S(1)}, u32[]{:S(2)}, u32[]{:S(2)}) async-start(bf16[4,128,128]{2,0,1:T(4,128)(2,1)} %copy.90), calls=%async_computation.2 | async-start | bytes 262144 | tf_op jit(solution)/shard_map/all_to_all | solution.py:124
where the time goes:
time: 211 us; the launch traced here: 210 us
  blocking collectives  163 us (77%)
  local copies, waits for them, and re-layouts  13 us (6%)
  waiting for transfers between devices  13 us (6%)
  starting transfers between devices  7.74 us (4%)
  matrix products  7.36 us (3%)
  other arithmetic  4.76 us (2%)
    all_gather x1, blocking collectives, on_device(): lax.all_gather(left_factor, 'row', axis=0, tiled=True)  44.6 us
    all_gather x1, blocking collectives, on_device(): full_bias = lax.all_gather(head_bias, 'row', axis=1, tiled=True)  42.5 us
    all_gather x1, blocking collectives, on_device(): lax.all_gather(right_factor, 'row', axis=0, tiled=True)  38.1 us
    all_gather x1, blocking collectives, on_device(): lax.all_gather(live_weights, 'row', axis=0, tiled=True)  37.9 us
    convert_element_type x2, local copies, waits for them, and re-layouts, on_device(): outer_flat.reshape(res_local * residue_total, opm_width * opm_width)  8.06 us
    all_to_all x1, waiting for transfers between devices, on_device(): lax.all_to_all(channel_sum, 'row', split_axis=1, concat_axis=0, tiled=True)  6.94 us
    all_to_all x1, waiting for transfers between devices, on_device(): lax.all_to_all(tri_right, 'row', split_axis=0, concat_axis=1, tiled=True)  6.06 us
  transfers between devices with their start and end apart: 3, of which 2 were waited for; matrix products, arithmetic and copies ran while one was open for 3% of the time, Pallas kernels for 0%

commit v1 on v0

--- a/solution.py
+++ b/solution.py
@@ -4,6 +4,18 @@
 from jax.sharding import PartitionSpec as P
 
 REL_MAX = 32
+
+
+def gather_by_bits(x, axis, dim):
+    ways, here, hop = (lax.axis_size(axis), lax.axis_index(axis), x.shape[dim])
+    line, have = (x, 1)
+    while have < ways:
+        line = jnp.concatenate(
+            [line, lax.ppermute(line, axis, [(d, (d - have) % ways) for d in range(ways)])],
+            axis=dim,
+        )
+        have = 2 * have
+    return jnp.roll(line, here * hop, axis=dim)
 
 
 def layer_normalize(values):
@@ -62,7 +74,7 @@
     live_weights = active_entry_mask.astype(jnp.bfloat16)
     left_all, right_all, live_all = (
         lax.all_gather(left_factor, "row", axis=0, tiled=True),
-        lax.all_gather(right_factor, "row", axis=0, tiled=True),
+        gather_by_bits(right_factor, "row", 0),
         lax.all_gather(live_weights, "row", axis=0, tiled=True),
     )
     left_cols = lax.dynamic_slice_in_dim(left_all, row_start * opm_width, res_local * opm_width, 1)

time: 211 us -> 199 us (0.943)
  blocking collectives: 163 us -> 121 us
  waiting for transfers between devices: 13 us -> 31.2 us
  starting transfers between devices: 7.74 us -> 15.3 us
  local copies, waits for them, and re-layouts: 13 us -> 15.9 us
    all_gather x1 -> x0, blocking collectives: 38.1 us -> none  [on_device(): lax.all_gather(right_factor, 'row', axis=0, tiled=True)]
    ppermute x0 -> x5, waiting for transfers between devices: none -> 18.2 us  [gather_by_bits(): lax.ppermute(line, axis, [(d, (d - have) % ways) for d in range(ways)])]
    ppermute x0 -> x5, starting transfers between devices: none -> 7.23 us  [gather_by_bits(): lax.ppermute(line, axis, [(d, (d - have) % ways) for d in range(ways)])]
  transfers between devices with their start and end apart: 3 -> 8, of which waited for: 2 -> 5; matrix products, arithmetic and copies ran while one was open for 3% -> 5% of each run, Pallas kernels for 0% -> 0%
where the time goes in v1:
time: 199 us
  blocking collectives  121 us (61%)
  waiting for transfers between devices  31.2 us (16%)
  local copies, waits for them, and re-layouts  15.9 us (8%)
  starting transfers between devices  15.3 us (8%)
  matrix products  8.05 us (4%)
  other arithmetic  5.62 us (3%)
    all_gather x1, blocking collectives, on_device(): lax.all_gather(left_factor, 'row', axis=0, tiled=True)  42.6 us
    all_gather x1, blocking collectives, on_device(): full_bias = lax.all_gather(head_bias, 'row', axis=1, tiled=True)  42.5 us
    all_gather x1, blocking collectives, on_device(): lax.all_gather(live_weights, 'row', axis=0, tiled=True)  36.4 us
    ppermute x5, waiting for transfers between devices, gather_by_bits(): lax.ppermute(line, axis, [(d, (d - have) % ways) for d in range(ways)])  18.2 us
    convert_element_type x2, local copies, waits for them, and re-layouts, on_device(): outer_flat.reshape(res_local * residue_total, opm_width * opm_width)  8.04 us
    ppermute x5, starting transfers between devices, gather_by_bits(): lax.ppermute(line, axis, [(d, (d - have) % ways) for d in range(ways)])  7.23 us
    all_to_all x1, waiting for transfers between devices, on_device(): lax.all_to_all(channel_sum, 'row', split_axis=1, concat_axis=0, tiled=True)  6.94 us
    all_to_all x1, waiting for transfers between devices, on_device(): lax.all_to_all(tri_right, 'row', split_axis=0, concat_axis=1, tiled=True)  6.07 us
  transfers between devices with their start and end apart: 8, of which 5 were waited for; matrix products, arithmetic and copies ran while one was open for 5% of the time, Pallas kernels for 0%

profile of v1, /device:TPU:0, one launch (start us, length us, event | category | flops | bytes accessed | tf_op | source)
XLA Modules:
  0.0 198.8 jit_solution(2463338795604930226)
XLA Ops:
  0.6 1.1 convert_reduce_fusion
  1.7 1.1 multiply_reduce_fusion.2
  2.8 1.0 multiply_convert_fusion.2
  3.9 0.7 convert_bitcast_fusion
  4.6 0.9 fusion.52
  5.8 6.4 %collective-permute-start = (bf16[2,4096]{1,0:T(2,128)(2,1)S(1)}, bf16[2,4096]{1,0:T(2,128)(2,1)S(1)}, u32[]{:S(2)}, u32[]{:S(2)}) collective-permute-start(bf16[2,4096]{1,0:T(2,128)(2,1)S(1)} %reshape.194), channel_id=1, source_target_pairs={{0,31},{1,0},{2,1},{3,2},{4,3},{5,4},{6,5},{7,6},{8,7},{9,8},{10,9... | collective-permute-start | bytes 49160 | tf_op jit(solution)/shard_map/ppermute | solution.py:14
  12.5 1.2 collective-permute-done
  13.7 0.6 collective-permute-start.1
  14.3 42.6 %all-gather = bf16[32,2,4096]{2,1,0:T(2,128)(2,1)S(1)} all-gather(bf16[1,2,4096]{2,1,0:T(2,128)(2,1)S(1)} %reshape.208), channel_id=1, replica_groups=mesh['grp'=1,'row'=32] {'row'}, dimensions={0}, use_global_device_ids=true | all-gather | bytes 540672 | tf_op jit(solution)/shard_map/all_gather | solution.py:76
  57.3 0.7 dynamic_slice.33
  58.1 0.7 dynamic_slice.34
  58.8 36.4 %all-gather.1 = bf16[32,2,128]{2,1,0:T(2,128)(2,1)S(1)} all-gather(bf16[1,2,128]{2,1,0:T(2,128)(2,1)S(1)} %get-tuple-element.101), channel_id=1, replica_groups=mesh['grp'=1,'row'=32] {'row'}, dimensions={0}, use_global_device_ids=true | all-gather | bytes 16896 | tf_op jit(solution)/shard_map/all_gather | solution.py:78
  95.6 5.4 %collective-permute-done.3 = bf16[16,4096]{1,0:T(8,128)(2,1)S(1)} collective-permute-done((bf16[16,4096]{1,0:T(8,128)(2,1)S(1)}, bf16[16,4096]{1,0:T(8,128)(2,1)S(1)}, u32[]{:S(2)}, u32[]{:S(2)}) %collective-permute-start.3) | collective-permute-done | bytes 131104 | tf_op jit(solution)/shard_map/ppermute | solution.py:14
  101.2 0.7 add_select_fusion
  102.0 1.0 reshape.209
  103.0 0.7 fusion.63
  103.7 11.5 %collective-permute-done.4 = bf16[32,4096]{1,0:T(8,128)(2,1)S(1)} collective-permute-done((bf16[32,4096]{1,0:T(8,128)(2,1)S(1)}, bf16[32,4096]{1,0:T(8,128)(2,1)S(1)}, u32[]{:S(2)}, u32[]{:S(2)}) %collective-permute-start.4) | collective-permute-done | bytes 262176 | tf_op jit(solution)/shard_map/ppermute | solution.py:14
  115.6 1.2 convolution_convert_fusion
  116.8 4.4 %convert_element_type.106 = bf16[4,32,128,32]{3,2,1,0:T(8,128)(2,1)} reshape(bf16[128,4096]{1,0:T(8,128)(2,1)S(1)} %convolution_convert_fusion) | data formatting | bytes 2097152 | tf_op jit(solution)/shard_map/convert_element_type | solution.py:87
  121.2 3.6 %copy.75 = bf16[4,128,32,32]{1,3,2,0:T(8,128)(2,1)S(1)} copy(bf16[4,128,32,32]{3,1,2,0:T(8,128)(2,1)} %bitcast.134) | data formatting | bytes 2097152 | tf_op jit(solution)/shard_map/convert_element_type | solution.py:87
  126.8 0.8 copy.83
  127.5 2.9 %all-to-all-start = ((bf16[128,4,128]{2,1,0:T(4,128)(2,1)}), bf16[128,4,128]{2,1,0:T(4,128)(2,1)S(1)}, u32[]{:S(2)}, u32[]{:S(2)}) async-start(bf16[128,4,128]{2,1,0:T(4,128)(2,1)} %bitcast.22), calls=%async_computation | async-start | bytes 262144 | tf_op jit(solution)/shard_map/all_to_all | solution.py:130
  131.2 0.8 copy.86
  132.1 42.5 %all_gather.11 = bf16[8,128,128]{2,0,1:T(8,128)(2,1)S(1)} all-gather(bf16[8,4,128]{2,0,1:T(8,128)(2,1)S(1)} %fusion.35), channel_id=1, replica_groups=mesh['grp'=1,'row'=32] {'row'}, dimensions={1}, use_global_device_ids=true | all-gather | bytes 270336 | tf_op jit(solution)/shard_map/all_gather | solution.py:118
  174.8 2.6 %all-to-all-start.1 = ((bf16[128,4,128]{2,1,0:T(4,128)(2,1)}), bf16[128,4,128]{2,1,0:T(4,128)(2,1)S(1)}, u32[]{:S(2)}, u32[]{:S(2)}) async-start(bf16[128,4,128]{2,1,0:T(4,128)(2,1)} %bitcast.27), calls=%async_computation.1 | async-start | bytes 262144 | tf_op jit(solution)/shard_map/all_to_all | solution.py:131
  177.5 2.0 while.10
  179.6 6.1 %all-to-all-done.1 = bf16[128,4,128]{2,1,0:T(4,128)(2,1)S(1)} async-done(((bf16[128,4,128]{2,1,0:T(4,128)(2,1)}), bf16[128,4,128]{2,1,0:T(4,128)(2,1)S(1)}, u32[]{:S(2)}, u32[]{:S(2)}) %all-to-all-start.1) | async-done | bytes 131104 | tf_op jit(solution)/shard_map/all_to_all | solution.py:131
  186.0 0.8 copy.90
  186.8 2.6 %all-to-all-start.2 = ((bf16[4,128,128]{2,0,1:T(4,128)(2,1)}), bf16[4,128,128]{2,0,1:T(4,128)(2,1)S(1)}, u32[]{:S(2)}, u32[]{:S(2)}) async-start(bf16[4,128,128]{2,0,1:T(4,128)(2,1)} %copy.90), calls=%async_computation.2 | async-start | bytes 262144 | tf_op jit(solution)/shard_map/all_to_all | solution.py:136
  189.8 0.9 fusion.33
  190.7 6.9 %all-to-all-done.2 = bf16[4,128,128]{2,0,1:T(4,128)(2,1)S(1)} async-done(((bf16[4,128,128]{2,0,1:T(4,128)(2,1)}), bf16[4,128,128]{2,0,1:T(4,128)(2,1)S(1)}, u32[]{:S(2)}, u32[]{:S(2)}) %all-to-all-start.2) | async-done | bytes 131104 | tf_op jit(solution)/shard_map/all_to_all | solution.py:136
  198.0 0.8 fusion.34
  (90 shorter events, 7.8 us)
Async XLA Ops:
  0.6 56.4 %copy-start = (bf16[256,1024]{1,0:T(8,128)(2,1)S(1)}, bf16[256,1024]{1,0:T(8,128)(2,1)}, u32[]{:S(2)}) copy-start(bf16[256,1024]{1,0:T(8,128)(2,1)} %param.24) | copy-start | bytes 1572868
  5.8 7.9 %collective-permute-start = (bf16[2,4096]{1,0:T(2,128)(2,1)S(1)}, bf16[2,4096]{1,0:T(2,128)(2,1)S(1)}, u32[]{:S(2)}, u32[]{:S(2)}) collective-permute-start(bf16[2,4096]{1,0:T(2,128)(2,1)S(1)} %reshape.194), channel_id=1, source_target_pairs={{0,31},{1,0},{2,1},{3,2},{4,3},{5,4},{6,5},{7,6},{8,7},{9,8},{10,9... | collective-permute-start | bytes 49160 | tf_op jit(solution)/shard_map/ppermute | solution.py:14
  13.7 43.2 %collective-permute-start.1 = (bf16[4,4096]{1,0:T(4,128)(2,1)S(1)}, bf16[4,4096]{1,0:T(4,128)(2,1)S(1)}, u32[]{:S(2)}, u32[]{:S(2)}) collective-permute-start(bf16[4,4096]{1,0:T(4,128)(2,1)S(1)} %pad_maximum_fusion.2), channel_id=1, source_target_pairs={{0,30},{1,31},{2,0},{3,1},{4,2},{5,3},{6,4},{7,5},{8,6},{9,7},{10,... | collective-permute-start | bytes 98312 | tf_op jit(solution)/shard_map/ppermute | solution.py:14
  56.9 38.3 %collective-permute-start.2 = (bf16[8,4096]{1,0:T(8,128)(2,1)S(1)}, bf16[8,4096]{1,0:T(8,128)(2,1)S(1)}, u32[]{:S(2)}, u32[]{:S(2)}) collective-permute-start(bf16[8,4096]{1,0:T(8,128)(2,1)S(1)} %pad_maximum_fusion.1), channel_id=1, source_target_pairs={{0,28},{1,29},{2,30},{3,31},{4,0},{5,1},{6,2},{7,3},{8,4},{9,5},{1... | collective-permute-start | bytes 196616 | tf_op jit(solution)/shard_map/ppermute | solution.py:14
  95.3 5.8 %collective-permute-start.3 = (bf16[16,4096]{1,0:T(8,128)(2,1)S(1)}, bf16[16,4096]{1,0:T(8,128)(2,1)S(1)}, u32[]{:S(2)}, u32[]{:S(2)}) collective-permute-start(bf16[16,4096]{1,0:T(8,128)(2,1)S(1)} %pad_maximum_fusion), channel_id=1, source_target_pairs={{0,24},{1,25},{2,26},{3,27},{4,28},{5,29},{6,30},{7,31},{8,0},{9,1... | collective-permute-start | bytes 393224 | tf_op jit(solution)/shard_map/ppermute | solution.py:14
  101.2 14.1 %collective-permute-start.4 = (bf16[32,4096]{1,0:T(8,128)(2,1)S(1)}, bf16[32,4096]{1,0:T(8,128)(2,1)S(1)}, u32[]{:S(2)}, u32[]{:S(2)}) collective-permute-start(bf16[32,4096]{1,0:T(8,128)(2,1)S(1)} %concatenate.25), channel_id=1, source_target_pairs={{0,16},{1,17},{2,18},{3,19},{4,20},{5,21},{6,22},{7,23},{8,24},{9,... | collective-permute-start | bytes 786440 | tf_op jit(solution)/shard_map/ppermute | solution.py:14
  116.7 8.1 %copy-start.10 = (bf16[1024,128]{1,0:T(8,128)(2,1)S(1)}, bf16[1024,128]{1,0:T(8,128)(2,1)}, u32[]{:S(2)}) copy-start(bf16[1024,128]{1,0:T(8,128)(2,1)} %param.23) | copy-start | bytes 786436
  121.2 4.1 %copy-start.4 = (bf16[4,128,128]{2,1,0:T(8,128)(2,1)S(1)}, bf16[4,128,128]{2,1,0:T(8,128)(2,1)}, u32[]{:S(2)}) copy-start(bf16[4,128,128]{2,1,0:T(8,128)(2,1)} %param.18) | copy-start | bytes 393220
  121.2 4.2 %copy-start.6 = (f32[66,128]{1,0:T(8,128)S(1)}, f32[66,128]{1,0:T(8,128)}, u32[]{:S(2)}) copy-start(f32[66,128]{1,0:T(8,128)} %param.21) | copy-start | bytes 101380
  121.2 5.1 %copy-start.3 = (bf16[128,512]{1,0:T(8,128)(2,1)S(1)}, bf16[128,512]{1,0:T(8,128)(2,1)}, u32[]{:S(2)}) copy-start(bf16[128,512]{1,0:T(8,128)(2,1)} %param.27) | copy-start | bytes 393220
  124.8 5.7 %copy-start.8 = (s32[2,128]{1,0:T(2,128)S(1)}, s32[2,128]{1,0:T(2,128)}, u32[]{:S(2)}) copy-start(s32[2,128]{1,0:T(2,128)} %param.17) | copy-start | bytes 3076
  124.8 5.7 %copy-start.2 = (bf16[256,256]{1,0:T(8,128)(2,1)S(1)}, bf16[256,256]{1,0:T(8,128)(2,1)}, u32[]{:S(2)}) copy-start(bf16[256,256]{1,0:T(8,128)(2,1)} %get-tuple-element.98) | copy-start | bytes 393220
  125.3 6.7 %copy-start.9 = (bf16[128,8]{0,1:T(8,128)(2,1)S(1)}, bf16[128,8]{0,1:T(8,128)(2,1)}, u32[]{:S(2)}) copy-start(bf16[128,8]{0,1:T(8,128)(2,1)} %param.26) | copy-start | bytes 6148
  127.5 47.3 %all-to-all-start = ((bf16[128,4,128]{2,1,0:T(4,128)(2,1)}), bf16[128,4,128]{2,1,0:T(4,128)(2,1)S(1)}, u32[]{:S(2)}, u32[]{:S(2)}) async-start(bf16[128,4,128]{2,1,0:T(4,128)(2,1)} %bitcast.22), calls=%async_computation | async-start | bytes 262144 | tf_op jit(solution)/shard_map/all_to_all | solution.py:130
  174.8 10.8 %all-to-all-start.1 = ((bf16[128,4,128]{2,1,0:T(4,128)(2,1)}), bf16[128,4,128]{2,1,0:T(4,128)(2,1)S(1)}, u32[]{:S(2)}, u32[]{:S(2)}) async-start(bf16[128,4,128]{2,1,0:T(4,128)(2,1)} %bitcast.27), calls=%async_computation.1 | async-start | bytes 262144 | tf_op jit(solution)/shard_map/all_to_all | solution.py:131
  177.4 12.0 %copy-start.11 = (bf16[128,128]{1,0:T(8,128)(2,1)S(1)}, bf16[128,128]{1,0:T(8,128)(2,1)}, u32[]{:S(2)}) copy-start(bf16[128,128]{1,0:T(8,128)(2,1)} %param.28) | copy-start | bytes 98308
  177.5 12.3 %copy-start.1 = (bf16[2,128,256]{2,1,0:T(8,128)(2,1)S(1)}, bf16[2,128,256]{2,1,0:T(8,128)(2,1)}, u32[]{:S(2)}) copy-start(bf16[2,128,256]{2,1,0:T(8,128)(2,1)} %param.16) | copy-start | bytes 393220
  177.5 12.3 %copy-start.5 = (bf16[256,256]{1,0:T(8,128)(2,1)S(1)}, bf16[256,256]{1,0:T(8,128)(2,1)}, u32[]{:S(2)}) copy-start(bf16[256,256]{1,0:T(8,128)(2,1)} %param.25) | copy-start | bytes 393220
  179.5 18.5 %copy-start.7 = (bf16[128,128]{1,0:T(8,128)(2,1)S(1)}, bf16[128,128]{1,0:T(8,128)(2,1)}, u32[]{:S(2)}) copy-start(bf16[128,128]{1,0:T(8,128)(2,1)} %param.29) | copy-start | bytes 98308
  186.8 10.8 %all-to-all-start.2 = ((bf16[4,128,128]{2,0,1:T(4,128)(2,1)}), bf16[4,128,128]{2,0,1:T(4,128)(2,1)S(1)}, u32[]{:S(2)}, u32[]{:S(2)}) async-start(bf16[4,128,128]{2,0,1:T(4,128)(2,1)} %copy.90), calls=%async_computation.2 | async-start | bytes 262144 | tf_op jit(solution)/shard_map/all_to_all | solution.py:136
